TPU v7x, 512 devices: a whole 4x8x8 slice. The times are simulated.
512 devices in a mesh: dp: 16 (over y, core), ulysses: 32 (over z, x).
Axes of the slice: x: 4, y: 8, z: 8, core: 2. Of those that a mesh axis runs over, the one named last changes fastest.
Arguments:
- query_rows: bfloat16 [65536, 4096], P(('dp', 'ulysses')), may hold values from -6 to 6
- key_rows: bfloat16 [65536, 512], P(('dp', 'ulysses')), may hold values from -6 to 6
- value_rows: bfloat16 [65536, 512], P(('dp', 'ulysses')), may hold values from -6 to 6
- grad_out: bfloat16 [65536, 4096], P(('dp', 'ulysses')), may hold values from -6 to 6
- doc_lengths: int32 [16, 12], replicated, may hold values from 1 to 2048, 4096 in all within a row
Outputs:
- attention: bfloat16 [65536, 4096], P(('dp', 'ulysses'))
- grad_queries: bfloat16 [65536, 4096], P(('dp', 'ulysses'))
- grad_keys: bfloat16 [65536, 512], P(('dp', 'ulysses'))
- grad_values: bfloat16 [65536, 512], P(('dp', 'ulysses'))
Inputs may be any that keep to these rules, and one draw needn't show every extreme that they name: `doc_lengths`: each row's 12 lengths sum to 4096, and the longest is 2048.
All inputs are finite; a program needn't handle non-finite values.
Results may differ from a plain program's by a relative error of at most 0.011.
Values may be sent and summed in bfloat16 or wider, within the bound.
A program may use at most 64 MiB of HBM per device.

v0:
```python
import math

import jax
import jax.numpy as jnp
from jax import lax
from jax.sharding import PartitionSpec as P

HD = 128
BLOCK = 512


masked_score = -1e30


def split_up(shard, dim, count):
    shape = shard.shape
    blocks = shard.reshape(*shape[:dim], count, shape[dim] // count, *shape[dim + 1 :])
    return jnp.moveaxis(blocks, dim, 0)


def cut_rows(length, count):
    unit = 8 if length >= 8 * count else 1
    return [length // unit * k // count * unit for k in range(1, count)]


def joined_along(blocks, dim):
    blocks = jnp.moveaxis(blocks, 0, dim)
    shape = blocks.shape
    return blocks.reshape(*shape[:dim], shape[dim] * shape[dim + 1], *shape[dim + 2 :])


def cut_exchange(shard, axis, pieces, split_dim, concat_dim):
    blocks = split_up(shard, split_dim, lax.axis_size(axis))
    widest = max(range(1, max(2, blocks.ndim - 1)), key=lambda d: blocks.shape[d])
    finished = []
    for section in jnp.split(blocks, cut_rows(blocks.shape[widest], pieces), axis=widest):
        if section.size:
            finished.append(lax.all_to_all(section, axis, split_axis=0, concat_axis=0, tiled=True))
    return joined_along(jnp.concatenate(finished, axis=widest), concat_dim)


def doc_starts(row_lengths, length):
    doc_ends = jnp.cumsum(row_lengths)
    positions = jnp.arange(length, dtype=jnp.int32)
    passed = (doc_ends[None, :] <= positions[:, None]).astype(jnp.int32)
    return jnp.sum(passed * row_lengths[None, :], axis=1)


def attend_head(query_head, key_head, value_head, grad_head, starts, owned_blocks, block_rows):
    length, head_width = query_head.shape
    blocks = length // block_rows
    score_scale = 1.0 / math.sqrt(head_width)
    offsets = jnp.arange(block_rows, dtype=jnp.int32)
    block_first = starts.reshape(blocks, block_rows)[:, 0]

    def forward_block(query_index, carried):
        output_rows, log_totals = carried
        row_start = query_index * block_rows
        query_block = lax.dynamic_slice_in_dim(query_head, row_start, block_rows, 0)
        first_key = lax.dynamic_slice_in_dim(starts, row_start, block_rows, 0)
        query_pos = row_start + offsets

        def key_step(key_index, status):
            key_start = key_index * block_rows
            needed = owned_blocks[query_index] & (
                key_start + block_rows - 1 >= block_first[query_index]
            )

            def key_update(status):
                running_max, running_sum, totals = status
                key_block = lax.dynamic_slice_in_dim(key_head, key_start, block_rows, 0)
                value_block = lax.dynamic_slice_in_dim(value_head, key_start, block_rows, 0)
                key_pos = key_start + offsets
                allowed = (key_pos[None, :] <= query_pos[:, None]) & (
                    key_pos[None, :] >= first_key[:, None]
                )
                scores = (
                    jnp.dot(query_block, key_block.T, preferred_element_type=jnp.float32)
                    * score_scale
                )
                scores = jnp.where(allowed, scores, masked_score)
                new_max = jnp.maximum(running_max, jnp.max(scores, axis=1))
                weights = jnp.where(allowed, jnp.exp(scores - new_max[:, None]), 0.0)
                factor = jnp.exp(running_max - new_max)
                running_sum = running_sum * factor + jnp.sum(weights, axis=1)
                totals = totals * factor[:, None] + jnp.dot(
                    weights.astype(jnp.bfloat16), value_block, preferred_element_type=jnp.float32
                )
                return (new_max, running_sum, totals)

            return lax.cond(needed, key_update, lambda unchanged: unchanged, status)

        start_status = (
            jnp.full((block_rows,), masked_score, dtype=jnp.float32),
            jnp.zeros((block_rows,), jnp.float32),
            jnp.zeros((block_rows, head_width), jnp.float32),
        )
        running_max, running_sum, totals = lax.fori_loop(0, query_index + 1, key_step, start_status)
        safe_sum = jnp.where(owned_blocks[query_index], running_sum, 1.0)
        output_block = (totals / safe_sum[:, None]).astype(jnp.bfloat16)
        output_rows = lax.dynamic_update_slice_in_dim(output_rows, output_block, row_start, 0)
        log_totals = lax.dynamic_update_slice_in_dim(
            log_totals, running_max + jnp.log(safe_sum), row_start, 0
        )
        return (output_rows, log_totals)

    output_rows, log_totals = lax.fori_loop(
        0,
        blocks,
        forward_block,
        (jnp.zeros((length, head_width), jnp.bfloat16), jnp.zeros((length,), jnp.float32)),
    )
    row_dots = jnp.sum(grad_head.astype(jnp.float32) * output_rows.astype(jnp.float32), axis=1)

    def backward_block(key_index, carried):
        grad_query, grad_key, grad_value = carried
        key_start = key_index * block_rows
        key_block = lax.dynamic_slice_in_dim(key_head, key_start, block_rows, 0)
        value_block = lax.dynamic_slice_in_dim(value_head, key_start, block_rows, 0)
        key_pos = key_start + offsets

        def query_step(query_index, status):
            row_start = query_index * block_rows
            needed = owned_blocks[query_index] & (
                key_start + block_rows - 1 >= block_first[query_index]
            )

            def query_update(status):
                query_sum, key_sum, value_sum = status
                query_block = lax.dynamic_slice_in_dim(query_head, row_start, block_rows, 0)
                grad_block = lax.dynamic_slice_in_dim(grad_head, row_start, block_rows, 0)
                log_block = lax.dynamic_slice_in_dim(log_totals, row_start, block_rows, 0)
                dot_block = lax.dynamic_slice_in_dim(row_dots, row_start, block_rows, 0)
                first_key = lax.dynamic_slice_in_dim(starts, row_start, block_rows, 0)
                query_pos = row_start + offsets
                allowed = (key_pos[None, :] <= query_pos[:, None]) & (
                    key_pos[None, :] >= first_key[:, None]
                )
                scores = (
                    jnp.dot(query_block, key_block.T, preferred_element_type=jnp.float32)
                    * score_scale
                )
                weights = jnp.where(allowed, jnp.exp(scores - log_block[:, None]), 0.0)
                weights_low = weights.astype(jnp.bfloat16)
                value_sum = value_sum + jnp.dot(
                    weights_low.T, grad_block, preferred_element_type=jnp.float32
                )
                grad_weights = jnp.dot(
                    grad_block, value_block.T, preferred_element_type=jnp.float32
                )
                grad_scores = (weights * (grad_weights - dot_block[:, None])).astype(jnp.bfloat16)
                key_sum = (
                    key_sum
                    + jnp.dot(grad_scores.T, query_block, preferred_element_type=jnp.float32)
                    * score_scale
                )
                query_now = (
                    lax.dynamic_slice_in_dim(query_sum, row_start, block_rows, 0)
                    + jnp.dot(grad_scores, key_block, preferred_element_type=jnp.float32)
                    * score_scale
                )
                query_sum = lax.dynamic_update_slice_in_dim(query_sum, query_now, row_start, 0)
                return (query_sum, key_sum, value_sum)

            return lax.cond(needed, query_update, lambda unchanged: unchanged, status)

        zeros_block = jnp.zeros((block_rows, head_width), jnp.float32)
        grad_query, key_sum, value_sum = lax.fori_loop(
            key_index, blocks, query_step, (grad_query, zeros_block, zeros_block)
        )
        grad_key = lax.dynamic_update_slice_in_dim(grad_key, key_sum, key_start, 0)
        grad_value = lax.dynamic_update_slice_in_dim(grad_value, value_sum, key_start, 0)
        return (grad_query, grad_key, grad_value)

    zero_rows = jnp.zeros((length, head_width), jnp.float32)
    grad_query, grad_key, grad_value = lax.fori_loop(
        0, blocks, backward_block, (zero_rows, zero_rows, zero_rows)
    )
    return (output_rows, grad_query.astype(jnp.bfloat16), grad_key, grad_value)


def per_device(query_rows, key_rows, value_rows, grad_out, doc_lengths):
    tokens = query_rows.shape[0]
    query_heads = query_rows.shape[1] // HD
    shared_heads = key_rows.shape[1] // HD
    group_size = query_heads // shared_heads
    split_query = query_rows.reshape(tokens, query_heads, HD)
    split_key = jnp.repeat(key_rows.reshape(tokens, shared_heads, HD), group_size, axis=1)
    split_value = jnp.repeat(value_rows.reshape(tokens, shared_heads, HD), group_size, axis=1)
    split_grad = grad_out.reshape(tokens, query_heads, HD)
    head_query, head_key, head_value, head_grad = (
        cut_exchange(split_query, "ulysses", 2, 1, 0),
        cut_exchange(split_key, "ulysses", 2, 1, 0),
        cut_exchange(split_value, "ulysses", 2, 1, 0),
        cut_exchange(split_grad, "ulysses", 2, 1, 0),
    )
    head_query = head_query[:, 0]
    head_key = head_key[:, 0]
    head_value = head_value[:, 0]
    head_grad = head_grad[:, 0]
    length = head_query.shape[0]
    blocks = length // BLOCK
    row_index = lax.axis_index("dp")
    own_starts = doc_starts(
        lax.dynamic_index_in_dim(doc_lengths, row_index, 0, keepdims=False), length
    )
    output_head, query_grad, key_grad, value_grad = attend_head(
        head_query,
        head_key,
        head_value,
        head_grad,
        own_starts,
        jnp.ones((blocks,), dtype=bool),
        BLOCK,
    )
    token_output, token_query, token_key, token_value = (
        lax.all_to_all(output_head[:, None], "ulysses", split_axis=0, concat_axis=1, tiled=True),
        lax.all_to_all(query_grad[:, None], "ulysses", split_axis=0, concat_axis=1, tiled=True),
        lax.all_to_all(
            key_grad.astype(jnp.bfloat16)[:, None],
            "ulysses",
            split_axis=0,
            concat_axis=1,
            tiled=True,
        ),
        lax.all_to_all(
            value_grad.astype(jnp.bfloat16)[:, None],
            "ulysses",
            split_axis=0,
            concat_axis=1,
            tiled=True,
        ),
    )
    attention = token_output.reshape(tokens, query_heads * HD)
    grad_queries = token_query.reshape(tokens, query_heads * HD)
    grad_keys = (
        jnp.sum(token_key.reshape(tokens, shared_heads, group_size, HD).astype(jnp.float32), axis=2)
        .astype(jnp.bfloat16)
        .reshape(tokens, shared_heads * HD)
    )
    grad_values = (
        jnp.sum(
            token_value.reshape(tokens, shared_heads, group_size, HD).astype(jnp.float32), axis=2
        )
        .astype(jnp.bfloat16)
        .reshape(tokens, shared_heads * HD)
    )
    return (attention, grad_queries, grad_keys, grad_values)


def solution(mesh):
    return jax.shard_map(
        per_device,
        mesh=mesh,
        in_specs=(
            P(("dp", "ulysses"), None),
            P(("dp", "ulysses"), None),
            P(("dp", "ulysses"), None),
            P(("dp", "ulysses"), None),
            P(),
        ),
        out_specs=(
            P(("dp", "ulysses"), None),
            P(("dp", "ulysses"), None),
            P(("dp", "ulysses"), None),
            P(("dp", "ulysses"), None),
        ),
        check_vma=False,
    )
```

profile of v0, /device:TPU:4, one launch (start us, length us, event | category | flops | bytes accessed | tf_op | source)
XLA Modules:
  0.0 538.9 jit_solution(5615610798688326298)
XLA Ops:
  2.7 30.2 %all_to_all.100 = bf16[32,64,1,128]{3,1,2,0:T(8,128)(2,1)} all-to-all(bf16[32,64,1,128]{3,1,2,0:T(8,128)(2,1)S(1)} %get-tuple-element.1592), channel_id=1, replica_groups=mesh['dp'=16,'ulysses'=32] {'ulysses'}, dimensions={0} | all-to-all | bytes 1048576 | tf_op jit(solution)/shard_map/all_to_all | solution.py:38
  39.6 14.8 %all-to-all-done.5 = bf16[32,64,1,128]{3,1,2,0:T(8,128)(2,1)S(1)} async-done(((bf16[32,64,1,128]{3,1,2,0:T(8,128)(2,1)}), bf16[32,64,1,128]{3,1,2,0:T(8,128)(2,1)S(1)}, u32[]{:S(2)}, u32[]{:S(2)}) %all-to-all-start.5) | async-done | bytes 524320 | tf_op jit(solution)/shard_map/all_to_all | solution.py:38
  54.4 21.4 %all_to_all.101 = bf16[32,64,1,128]{3,1,2,0:T(8,128)(2,1)} all-to-all(bf16[32,64,1,128]{3,1,2,0:T(8,128)(2,1)S(1)} %get-tuple-element.1594), channel_id=1, replica_groups=mesh['dp'=16,'ulysses'=32] {'ulysses'}, dimensions={0} | all-to-all | bytes 1048576 | tf_op jit(solution)/shard_map/all_to_all | solution.py:38
  83.7 13.7 %all-to-all-done.3 = bf16[32,64,1,128]{3,1,2,0:T(8,128)(2,1)} async-done(((bf16[32,64,1,128]{3,1,2,0:T(8,128)(2,1)}), bf16[32,64,1,128]{3,1,2,0:T(8,128)(2,1)}, u32[]{:S(2)}, u32[]{:S(2)}) %all-to-all-start.3) | async-done | bytes 524320 | tf_op jit(solution)/shard_map/all_to_all | solution.py:38
  104.2 14.8 %all-to-all-done = bf16[32,64,1,128]{3,1,2,0:T(8,128)(2,1)S(1)} async-done(((bf16[32,64,1,128]{3,1,2,0:T(8,128)(2,1)}), bf16[32,64,1,128]{3,1,2,0:T(8,128)(2,1)S(1)}, u32[]{:S(2)}, u32[]{:S(2)}) %all-to-all-start) | async-done | bytes 524320 | tf_op jit(solution)/shard_map/all_to_all | solution.py:38
  127.8 12.9 %all-to-all-done.1 = bf16[32,64,1,128]{3,1,2,0:T(8,128)(2,1)} async-done(((bf16[32,64,1,128]{3,1,2,0:T(8,128)(2,1)}), bf16[32,64,1,128]{3,1,2,0:T(8,128)(2,1)}, u32[]{:S(2)}, u32[]{:S(2)}) %all-to-all-start.1) | async-done | bytes 524320 | tf_op jit(solution)/shard_map/all_to_all | solution.py:38
  168.0 98.3 %while.164 = (s32[]{:T(128)}, bf16[4096,128]{1,0:T(8,128)(2,1)S(1)}, f32[4096]{0:T(1024)S(1)}, s32[4096]{0:T(1024)S(1)}, bf16[4096,128]{1,0:T(8,128)(2,1)S(1)}, ...) while((s32[]{:T(128)}, bf16[4096,128]{1,0:T(8,128)(2,1)S(1)}, ...), condition=%wide.region_9.10_spmd.clone.clone, body=%wide.region_2.9_spmd.clone.clone.sunk | while | flops 139201024 | bytes 5057256 | solution.py:107
  201.7 12.7 %while.167 = (s32[]{:T(128)}, f32[512]{0:T(512)S(1)}, f32[512]{0:T(512)S(1)}, f32[512,128]{1,0:T(8,128)S(1)}, s32[]{:T(128)}, /*index=5*/s32[1]{0:T(128)}, s32[5...) while((s32[]{:T(128)}, f32[512]{0:T(512)S(1)}, ...), condition=%wide.region_8.8_spmd, body=%wide.region_3.7_spmd.sunk | while | flops 139068928 | bytes 4118889 | solution.py:98
  215.5 16.5 %while.167 = (s32[]{:T(128)}, f32[512]{0:T(512)S(1)}, f32[512]{0:T(512)S(1)}, f32[512,128]{1,0:T(8,128)S(1)}, s32[]{:T(128)}, /*index=5*/s32[1]{0:T(128)}, s32[5...) while((s32[]{:T(128)}, f32[512]{0:T(512)S(1)}, ...), condition=%wide.region_8.8_spmd, body=%wide.region_3.7_spmd.sunk | while | flops 139068928 | bytes 4118889 | solution.py:98
  233.1 20.2 %while.167 = (s32[]{:T(128)}, f32[512]{0:T(512)S(1)}, f32[512]{0:T(512)S(1)}, f32[512,128]{1,0:T(8,128)S(1)}, s32[]{:T(128)}, /*index=5*/s32[1]{0:T(128)}, s32[5...) while((s32[]{:T(128)}, f32[512]{0:T(512)S(1)}, ...), condition=%wide.region_8.8_spmd, body=%wide.region_3.7_spmd.sunk | while | flops 139068928 | bytes 4118889 | solution.py:98
  254.4 11.5 %while.167 = (s32[]{:T(128)}, f32[512]{0:T(512)S(1)}, f32[512]{0:T(512)S(1)}, f32[512,128]{1,0:T(8,128)S(1)}, s32[]{:T(128)}, /*index=5*/s32[1]{0:T(128)}, s32[5...) while((s32[]{:T(128)}, f32[512]{0:T(512)S(1)}, ...), condition=%wide.region_8.8_spmd, body=%wide.region_3.7_spmd.sunk | while | flops 139068928 | bytes 4118889 | solution.py:98
  272.9 9.8 %all-to-all-start.6 = ((bf16[32,2,8192]{2,1,0:T(2,128)(2,1)}), bf16[32,2,8192]{2,1,0:T(2,128)(2,1)}, u32[]{:S(2)}, u32[]{:S(2)}) async-start(bf16[32,2,8192]{2,1,0:T(2,128)(2,1)} %reshape.86), calls=%async_computation.6 | async-start | bytes 2097152 | tf_op jit(solution)/shard_map/all_to_all | solution.py:217
  284.3 145.7 %while.166 = (s32[]{:T(128)}, f32[4096,128]{1,0:T(8,128)}, bf16[4096,128]{1,0:T(8,128)(2,1)}, bf16[4096,128]{1,0:T(8,128)(2,1)}, bf16[4096,128]{1,0:T(8,128)(2,1...) while((s32[]{:T(128)}, f32[4096,128]{1,0:T(8,128)}, ...), condition=%wide.region_16.17_spmd.clone.clone, body=%wide.region_11.16_spmd.clone.clone.sunk | while | flops 338494464 | bytes 9337730 | solution.py:176
  286.2 17.8 %while.168 = (s32[]{:T(128)}, f32[4096,128]{1,0:T(8,128)}, f32[512,128]{1,0:T(8,128)S(1)}, f32[512,128]{1,0:T(8,128)S(1)}, s32[8]{0:T(128)S(1)}, /*index=5*/s32[...) while((s32[]{:T(128)}, f32[4096,128]{1,0:T(8,128)}, ...), condition=%wide.region_15.15_spmd, body=%wide.region_12.14_spmd.sunk | while | flops 338493952 | bytes 7236059 | solution.py:168
  306.6 16.5 %while.168 = (s32[]{:T(128)}, f32[4096,128]{1,0:T(8,128)}, f32[512,128]{1,0:T(8,128)S(1)}, f32[512,128]{1,0:T(8,128)S(1)}, s32[8]{0:T(128)S(1)}, /*index=5*/s32[...) while((s32[]{:T(128)}, f32[4096,128]{1,0:T(8,128)}, ...), condition=%wide.region_15.15_spmd, body=%wide.region_12.14_spmd.sunk | while | flops 338493952 | bytes 7236059 | solution.py:168
  325.8 26.3 %while.168 = (s32[]{:T(128)}, f32[4096,128]{1,0:T(8,128)}, f32[512,128]{1,0:T(8,128)S(1)}, f32[512,128]{1,0:T(8,128)S(1)}, s32[8]{0:T(128)S(1)}, /*index=5*/s32[...) while((s32[]{:T(128)}, f32[4096,128]{1,0:T(8,128)}, ...), condition=%wide.region_15.15_spmd, body=%wide.region_12.14_spmd.sunk | while | flops 338493952 | bytes 7236059 | solution.py:168
  354.7 21.3 %while.168 = (s32[]{:T(128)}, f32[4096,128]{1,0:T(8,128)}, f32[512,128]{1,0:T(8,128)S(1)}, f32[512,128]{1,0:T(8,128)S(1)}, s32[8]{0:T(128)S(1)}, /*index=5*/s32[...) while((s32[]{:T(128)}, f32[4096,128]{1,0:T(8,128)}, ...), condition=%wide.region_15.15_spmd, body=%wide.region_12.14_spmd.sunk | while | flops 338493952 | bytes 7236059 | solution.py:168
  378.6 16.3 %while.168 = (s32[]{:T(128)}, f32[4096,128]{1,0:T(8,128)}, f32[512,128]{1,0:T(8,128)S(1)}, f32[512,128]{1,0:T(8,128)S(1)}, s32[8]{0:T(128)S(1)}, /*index=5*/s32[...) while((s32[]{:T(128)}, f32[4096,128]{1,0:T(8,128)}, ...), condition=%wide.region_15.15_spmd, body=%wide.region_12.14_spmd.sunk | while | flops 338493952 | bytes 7236059 | solution.py:168
  397.5 11.3 %while.168 = (s32[]{:T(128)}, f32[4096,128]{1,0:T(8,128)}, f32[512,128]{1,0:T(8,128)S(1)}, f32[512,128]{1,0:T(8,128)S(1)}, s32[8]{0:T(128)S(1)}, /*index=5*/s32[...) while((s32[]{:T(128)}, f32[4096,128]{1,0:T(8,128)}, ...), condition=%wide.region_15.15_spmd, body=%wide.region_12.14_spmd.sunk | while | flops 338493952 | bytes 7236059 | solution.py:168
  411.5 10.0 %while.168 = (s32[]{:T(128)}, f32[4096,128]{1,0:T(8,128)}, f32[512,128]{1,0:T(8,128)S(1)}, f32[512,128]{1,0:T(8,128)S(1)}, s32[8]{0:T(128)S(1)}, /*index=5*/s32[...) while((s32[]{:T(128)}, f32[4096,128]{1,0:T(8,128)}, ...), condition=%wide.region_15.15_spmd, body=%wide.region_12.14_spmd.sunk | while | flops 338493952 | bytes 7236059 | solution.py:168
  433.8 9.8 %all-to-all-start.11 = ((bf16[32,2,8192]{2,1,0:T(2,128)(2,1)}), bf16[32,2,8192]{2,1,0:T(2,128)(2,1)S(1)}, u32[]{:S(2)}, u32[]{:S(2)}) async-start(bf16[32,2,8192]{2,1,0:T(2,128)(2,1)} %reshape.92), calls=%async_computation.11 | async-start | bytes 2097152 | tf_op jit(solution)/shard_map/all_to_all | solution.py:226
  447.9 21.7 %all-to-all-done.11 = bf16[32,2,8192]{2,1,0:T(2,128)(2,1)S(1)} async-done(((bf16[32,2,8192]{2,1,0:T(2,128)(2,1)}), bf16[32,2,8192]{2,1,0:T(2,128)(2,1)S(1)}, u32[]{:S(2)}, u32[]{:S(2)}) %all-to-all-start.11) | async-done | bytes 1048608 | tf_op jit(solution)/shard_map/all_to_all | solution.py:226
  477.9 23.3 %all-to-all-done.10 = bf16[32,2,8192]{2,1,0:T(2,128)(2,1)} async-done(((bf16[32,2,8192]{2,1,0:T(2,128)(2,1)}), bf16[32,2,8192]{2,1,0:T(2,128)(2,1)}, u32[]{:S(2)}, u32[]{:S(2)}) %all-to-all-start.10) | async-done | bytes 1048608 | tf_op jit(solution)/shard_map/all_to_all | solution.py:219
  521.1 11.4 %all-to-all-done.9 = bf16[32,2,8192]{2,1,0:T(2,128)(2,1)} async-done(((bf16[32,2,8192]{2,1,0:T(2,128)(2,1)}), bf16[32,2,8192]{2,1,0:T(2,128)(2,1)}, u32[]{:S(2)}, u32[]{:S(2)}) %all-to-all-start.9) | async-done | bytes 1048608 | tf_op jit(solution)/shard_map/all_to_all | solution.py:218
  (685 shorter events, 481.9 us)
Async XLA Ops:
  1.8 36.6 %copy-start.15 = (bf16[128,512]{1,0:T(8,128)(2,1)S(1)}, bf16[128,512]{1,0:T(8,128)(2,1)}, u32[]{:S(2)}) copy-start(bf16[128,512]{1,0:T(8,128)(2,1)} %param.18) | copy-start | bytes 393220
  32.9 21.5 %all-to-all-start.5 = ((bf16[32,64,1,128]{3,1,2,0:T(8,128)(2,1)}), bf16[32,64,1,128]{3,1,2,0:T(8,128)(2,1)S(1)}, u32[]{:S(2)}, u32[]{:S(2)}) async-start(bf16[32,64,1,128]{3,1,2,0:T(8,128)(2,1)} %get-tuple-element.1593), calls=%async_computation.5 | async-start | bytes 1048576 | tf_op jit(solution)/shard_map/all_to_all | solution.py:38
  38.7 42.8 %copy-start.13 = (bf16[128,4096]{1,0:T(8,128)(2,1)S(1)}, bf16[128,4096]{1,0:T(8,128)(2,1)}, u32[]{:S(2)}) copy-start(bf16[128,4096]{1,0:T(8,128)(2,1)} %param.17) | copy-start | bytes 3145732
  54.4 21.4 %copy-start.8 = (bf16[32,64,1,128]{3,1,2,0:T(8,128)(2,1)}, bf16[32,64,1,128]{3,1,2,0:T(8,128)(2,1)S(1)}, u32[]{:S(2)}) copy-start(bf16[32,64,1,128]{3,1,2,0:T(8,128)(2,1)S(1)} %all-to-all-done.5) | copy-start | bytes 1572868
  75.8 21.6 %all-to-all-start.3 = ((bf16[32,64,1,128]{3,1,2,0:T(8,128)(2,1)}), bf16[32,64,1,128]{3,1,2,0:T(8,128)(2,1)}, u32[]{:S(2)}, u32[]{:S(2)}) async-start(bf16[32,64,1,128]{3,1,2,0:T(8,128)(2,1)} %get-tuple-element.1595), calls=%async_computation.3 | async-start | bytes 1048576 | tf_op jit(solution)/shard_map/all_to_all | solution.py:38
  83.7 41.8 %copy-start.14 = (bf16[128,4096]{1,0:T(8,128)(2,1)S(1)}, bf16[128,4096]{1,0:T(8,128)(2,1)}, u32[]{:S(2)}) copy-start(bf16[128,4096]{1,0:T(8,128)(2,1)} %param.20) | copy-start | bytes 3145732
  97.5 21.5 %all-to-all-start = ((bf16[32,64,1,128]{3,1,2,0:T(8,128)(2,1)}), bf16[32,64,1,128]{3,1,2,0:T(8,128)(2,1)S(1)}, u32[]{:S(2)}, u32[]{:S(2)}) async-start(bf16[32,64,1,128]{3,1,2,0:T(8,128)(2,1)} %copy.68), calls=%async_computation | async-start | bytes 1048576 | tf_op jit(solution)/shard_map/all_to_all | solution.py:38
  119.0 6.3 %copy-start.11 = (bf16[32,64,1,128]{3,1,2,0:T(8,128)(2,1)}, bf16[32,64,1,128]{3,1,2,0:T(8,128)(2,1)S(1)}, u32[]{:S(2)}) copy-start(bf16[32,64,1,128]{3,1,2,0:T(8,128)(2,1)S(1)} %all-to-all-done) | copy-start | bytes 1572868
  119.0 21.6 %all-to-all-start.1 = ((bf16[32,64,1,128]{3,1,2,0:T(8,128)(2,1)}), bf16[32,64,1,128]{3,1,2,0:T(8,128)(2,1)}, u32[]{:S(2)}, u32[]{:S(2)}) async-start(bf16[32,64,1,128]{3,1,2,0:T(8,128)(2,1)} %copy.69), calls=%async_computation.1 | async-start | bytes 1048576 | tf_op jit(solution)/shard_map/all_to_all | solution.py:38
  140.6 21.5 %all-to-all-start.7 = ((bf16[32,64,1,128]{3,1,2,0:T(8,128)(2,1)}), bf16[32,64,1,128]{3,1,2,0:T(8,128)(2,1)S(1)}, u32[]{:S(2)}, u32[]{:S(2)}) async-start(bf16[32,64,1,128]{3,1,2,0:T(8,128)(2,1)} %copy.75), calls=%async_computation.7 | async-start | bytes 1048576 | tf_op jit(solution)/shard_map/all_to_all | solution.py:38
  147.4 2.3 copy-start.7
  147.4 2.3 copy-start.9
  148.4 2.3 copy-start.10
  149.7 3.2 copy-start.12
  162.2 5.6 %copy-start.6 = (bf16[32,64,1,128]{3,1,2,0:T(8,128)(2,1)}, bf16[32,64,1,128]{3,1,2,0:T(8,128)(2,1)S(1)}, u32[]{:S(2)}) copy-start(bf16[32,64,1,128]{3,1,2,0:T(8,128)(2,1)S(1)} %all-to-all-done.7) | copy-start | bytes 1572868
  162.2 104.1 %all-to-all-start.8 = ((bf16[32,64,1,128]{3,1,2,0:T(8,128)(2,1)}), bf16[32,64,1,128]{3,1,2,0:T(8,128)(2,1)}, u32[]{:S(2)}, u32[]{:S(2)}) async-start(bf16[32,64,1,128]{3,1,2,0:T(8,128)(2,1)} %copy.76), calls=%async_computation.8 | async-start | bytes 1048576 | tf_op jit(solution)/shard_map/all_to_all | solution.py:38
  272.9 160.8 %all-to-all-start.6 = ((bf16[32,2,8192]{2,1,0:T(2,128)(2,1)}), bf16[32,2,8192]{2,1,0:T(2,128)(2,1)}, u32[]{:S(2)}, u32[]{:S(2)}) async-start(bf16[32,2,8192]{2,1,0:T(2,128)(2,1)} %reshape.86), calls=%async_computation.6 | async-start | bytes 2097152 | tf_op jit(solution)/shard_map/all_to_all | solution.py:217
  432.6 10.9 %copy-start.3 = (bf16[4096,128]{1,0:T(8,128)(2,1)S(1)}, bf16[4096,128]{1,0:T(8,128)(2,1)}, u32[]{:S(2)}) copy-start(bf16[4096,128]{1,0:T(8,128)(2,1)} %get-tuple-element.1366) | copy-start | bytes 3145732
  433.8 35.9 %all-to-all-start.11 = ((bf16[32,2,8192]{2,1,0:T(2,128)(2,1)}), bf16[32,2,8192]{2,1,0:T(2,128)(2,1)S(1)}, u32[]{:S(2)}, u32[]{:S(2)}) async-start(bf16[32,2,8192]{2,1,0:T(2,128)(2,1)} %reshape.92), calls=%async_computation.11 | async-start | bytes 2097152 | tf_op jit(solution)/shard_map/all_to_all | solution.py:226
  445.6 29.6 %copy-start.1 = (f32[4096,128]{1,0:T(8,128)S(1)}, f32[4096,128]{1,0:T(8,128)}, u32[]{:S(2)}) copy-start(f32[4096,128]{1,0:T(8,128)} %get-tuple-element.1365) | copy-start | bytes 6291460
  469.6 5.6 %copy-start.4 = (bf16[32,2,8192]{2,1,0:T(2,128)(2,1)}, bf16[32,2,8192]{2,1,0:T(2,128)(2,1)S(1)}, u32[]{:S(2)}) copy-start(bf16[32,2,8192]{2,1,0:T(2,128)(2,1)S(1)} %all-to-all-done.11) | copy-start | bytes 3145732
  469.6 31.6 %all-to-all-start.10 = ((bf16[32,2,8192]{2,1,0:T(2,128)(2,1)}), bf16[32,2,8192]{2,1,0:T(2,128)(2,1)}, u32[]{:S(2)}, u32[]{:S(2)}) async-start(bf16[32,2,8192]{2,1,0:T(2,128)(2,1)} %reshape.90), calls=%async_computation.10 | async-start | bytes 2097152 | tf_op jit(solution)/shard_map/all_to_all | solution.py:219
  501.2 31.3 %all-to-all-start.9 = ((bf16[32,2,8192]{2,1,0:T(2,128)(2,1)}), bf16[32,2,8192]{2,1,0:T(2,128)(2,1)}, u32[]{:S(2)}, u32[]{:S(2)}) async-start(bf16[32,2,8192]{2,1,0:T(2,128)(2,1)} %reshape.88), calls=%async_computation.9 | async-start | bytes 2097152 | tf_op jit(solution)/shard_map/all_to_all | solution.py:218
  511.3 2.0 copy-start.5
  (2 other events, 1.9 us)
where the time goes:
time: 543 us; the launch traced here: 539 us
  matrix products  130 us (24%)
  waiting for transfers between devices  121 us (22%)
  local copies, waits for them, and re-layouts  96 us (18%)
  starting transfers between devices  64.4 us (12%)
  blocking collectives  51.6 us (10%)
  loops' own time  50.3 us (9%)
  other arithmetic  25 us (5%)
    all_to_all x6, waiting for transfers between devices, cut_exchange(): lax.all_to_all(section, axis, split_axis=0, concat_axis=0, tiled=True)  64.4 us
    all_to_all x2, blocking collectives, cut_exchange(): lax.all_to_all(section, axis, split_axis=0, concat_axis=0, tiled=True)  51.6 us
    dot_general x21, matrix products, query_update(): jnp.dot(grad_scores, key_block, preferred_element_type=jnp.float32)  41.1 us
    all_to_all x6, starting transfers between devices, cut_exchange(): lax.all_to_all(section, axis, split_axis=0, concat_axis=0, tiled=True)  33.6 us
    dot_general x21, matrix products, key_update(): jnp.dot(weights.astype(jnp.bfloat16), value_block, preferred_element_type...  30.4 us
    unnamed x51, local copies, waits for them, and re-layouts  29.6 us
    dot_general x21, matrix products, key_update(): jnp.dot(query_block, key_block.T, preferred_element_type=jnp.float32)  27.1 us
    another operation x8, loops' own time, backward_block(): lax.fori_loop(key_index, blocks, query_step, (grad_query, zeros_block, ze...  23.5 us
  transfers between devices with their start and end apart: 10, of which 8 were waited for; matrix products, arithmetic and copies ran while one was open for 44% of the time, Pallas kernels for 0%

commit v1 on v0

v1 whole, which is shorter than its diff:
```python
import math

import jax
import jax.numpy as jnp
from jax import lax
from jax.experimental import pallas as pl
from jax.experimental.pallas import tpu as pltpu
from jax.sharding import PartitionSpec as P

HD = 128
XS = 4
ZS = 8
SH = 128
BLK = XS * SH
NB = 5
GRP = 8
DOCS = 12
HALF = 256
SCALE = 1.0 / math.sqrt(HD)
LOG2 = SCALE * math.log2(math.e)
BIG = -(2.0**100)
MESH = pl.DeviceIdType.MESH
F32 = jnp.float32
BF16 = jnp.bfloat16


def dot(a, b):
    return jnp.dot(a, b, preferred_element_type=F32)


def aligned(index, size):
    return pl.ds(pl.multiple_of(index * size, size), size)


def query_range(b, c):
    if b == NB - 1:
        return (0, BLK) if c < 2 else (HALF, BLK)
    if b == 0:
        return (0, HALF) if c < 2 else (0, BLK)
    return (0, BLK)


def backward_tiles(b):
    if b == NB - 1:
        return [(0, HALF, 0, BLK), (HALF, HALF, HALF, HALF)]
    if b == 0:
        return [(0, HALF, 0, HALF), (HALF, HALF, 0, BLK)]
    return [(0, BLK, 0, BLK)]


def kernel(
    dl, q_in, k_in, v_in, g_in,
    att, dq_out, dk_out, dv_out,
    kw, vw, qn, gn, on, dqn,
    qx, gT, kx, kT, vTx, prob, acc, maxes, sums, dqT, scal, s_a, s_b,
    dkv, dkv_own, ring_in, ring_out, last,
    in_send, in_recv, loc, hop_send, hop_recv, o_send, o_recv, dq_send, dq_recv,
    red_send, red_recv, fin_send, fin_recv,
):
    dp = lax.axis_index("dp")
    u = lax.axis_index("ulysses")
    x = lax.rem(u, XS)
    z = lax.div(u, XS)
    peer_x = [lax.rem(x + r, XS) for r in range(XS)]
    peers = [(dp, z * XS + peer_x[r]) for r in range(XS)]
    up = (dp, lax.rem(z + 1, ZS) * XS + x)
    down = (dp, lax.rem(z + ZS - 1, ZS) * XS + x)

    def remote(src, dst, send, recv, device):
        return pltpu.make_async_remote_copy(
            src_ref=src, dst_ref=dst, send_sem=send, recv_sem=recv,
            device_id=device, device_id_type=MESH,
        )

    barrier = pltpu.get_barrier_semaphore()
    for device in (peers[1], peers[2], peers[3], up, down):
        pl.semaphore_signal(barrier, inc=1, device_id=device, device_id_type=MESH)
    pl.semaphore_wait(barrier, 5)

    mine = aligned(x, SH)
    wide = GRP * HD
    moves = (
        (k_in, HD, kw.at[NB - 1]),
        (v_in, HD, vw.at[NB - 1]),
        (q_in, wide, qn),
        (g_in, wide, gn),
    )
    arrive = []
    local = []
    for n, (src, width, dst) in enumerate(moves):
        row = []
        for r in (1, 3, 2):
            copy = remote(
                src.at[:, aligned(peer_x[r], width)], dst.at[mine, :],
                in_send.at[n, r], in_recv.at[n, r], peers[r],
            )
            copy.start()
            row.append(copy)
        own = pltpu.make_async_copy(src.at[:, aligned(x, width)], dst.at[mine, :], loc.at[n])
        own.start()
        arrive.append(row)
        local.append(own)

    def arrived(n):
        local[n].wait()
        for copy in arrive[n]:
            copy.wait()

    hops = {}

    def hop(b):
        hops[b] = [
            remote(w.at[b], w.at[b - 1], hop_send.at[n, b], hop_recv.at[n, b], up)
            for n, w in enumerate((kw, vw))
        ]
        for copy in hops[b]:
            copy.start()

    def hopped(b):
        for copy in hops[b]:
            copy.wait()

    base = (z - (NB - 1)) * BLK
    lane = lax.broadcasted_iota(jnp.int32, (1, HD), 1)
    key_lo = jnp.full((1, HD), 1 << 30, jnp.int32)
    key_hi = jnp.full((1, HD), -(1 << 30), jnp.int32)
    sub = lax.broadcasted_iota(jnp.int32, (HD, BLK), 0)
    pos = lax.broadcasted_iota(jnp.int32, (HD, BLK), 1) + (NB - 1) * BLK
    bias = jnp.where(sub == DOCS, BIG, 0.0).astype(F32)
    first = -base
    for d in range(DOCS):
        end = first + dl[dp, d]
        key_lo = jnp.where(lane == d, first, key_lo)
        key_hi = jnp.where(lane == d, end, key_hi)
        inside = (pos >= first) & (pos < end)
        bias = jnp.where((sub == d) & jnp.logical_not(inside), BIG, bias)
        first = end
    key_lo = jnp.where(lane == DOCS, -(1 << 30), key_lo)
    key_hi = jnp.where(lane == DOCS, -base, key_hi)
    bias = bias.astype(BF16)
    for h in range(GRP):
        qx[h, HD:, :] = bias

    def prepare(b):
        j = lax.broadcasted_iota(jnp.int32, (BLK, HD), 0) + b * BLK
        kx[b, :, HD:] = jnp.where((j >= key_lo) & (j < key_hi), 1.0, 0.0).astype(BF16)
        kx[b, :, 0:HD] = kw[b]
        kT[b] = kw[b].T
        vTx[b, 0:HD, :] = vw[b].T
        vTx[b, HD:, :] = jnp.ones((16, BLK), BF16)

    def scores(b, h, to, c, tops):
        q0, q1 = query_range(b, c)
        rows = slice(c * SH, c * SH + SH)
        s = dot(kx[b, rows, :], qx[h, :, q0:q1])
        if b == NB - 1:
            j = lax.broadcasted_iota(jnp.int32, (SH, q1 - q0), 0) + c * SH
            i = lax.broadcasted_iota(jnp.int32, (SH, q1 - q0), 1) + q0
            s = jnp.where(j <= i, s, BIG)
        to[rows, q0:q1] = s
        top = jnp.max(s, axis=0, keepdims=True)
        for n, lo in enumerate((0, HALF)):
            if q0 <= lo and lo + HALF <= q1:
                t = top[:, lo - q0 : lo - q0 + HALF]
                tops[n] = t if tops[n] is None else jnp.maximum(tops[n], t)

    def put_tops(b, h, tops):
        for n in range(2):
            maxes[h, b : b + 1, n * HALF : n * HALF + HALF] = tops[n]

    def forward(b):
        tops = [None, None]
        for c in range(4):
            scores(b, 0, s_a, c, tops)
        put_tops(b, 0, tops)

        def one(h, now, later):
            ahead = jnp.minimum(h + 1, GRP - 1)
            top = maxes[h, b : b + 1, :]
            tops = [None, None]
            outs = [None, None]
            held = None
            for c in range(4):
                scores(b, ahead, later, c, tops)
                q0, q1 = query_range(b, c)
                rows = slice(c * SH, c * SH + SH)
                p = jnp.exp2((now[rows, q0:q1] - top[:, q0:q1]) * LOG2).astype(BF16)
                prob[h, b, rows, q0:q1] = p
                if c % 2:
                    pair = jnp.concatenate([held, p], axis=0)
                    t = dot(vTx[b, :, c * SH - SH : c * SH + SH], pair)
                    for n, lo in enumerate((0, HALF)):
                        if q0 <= lo and lo + HALF <= q1:
                            part = t[:, lo - q0 : lo - q0 + HALF]
                            outs[n] = part if outs[n] is None else outs[n] + part
                held = p
            put_tops(b, ahead, tops)
            for n in range(2):
                qs = slice(n * HALF, n * HALF + HALF)
                out, total, peak = outs[n][0:HD], outs[n][HD : HD + 1], top[:, qs]
                if b == NB - 1:
                    maxes[h, NB : NB + 1, qs] = peak
                    sums[h, 0:1, qs] = total
                    acc[h, :, qs] = out
                else:
                    old = maxes[h, NB : NB + 1, qs]
                    new = jnp.maximum(old, peak)
                    keep = jnp.exp2((old - new) * LOG2)
                    add = jnp.exp2((peak - new) * LOG2)
                    maxes[h, NB : NB + 1, qs] = new
                    sums[h, 0:1, qs] = sums[h, 0:1, qs] * keep + total * add
                    acc[h, :, qs] = acc[h, :, qs] * keep + out * add

        def two(pair, _):
            one(pair * 2, s_a, s_b)
            one(pair * 2 + 1, s_b, s_a)
            return 0

        lax.fori_loop(0, GRP // 2, two, 0)

    def backward(b, h, into):
        cols = aligned(h, HD)
        for n, (k0, kl, q0, ql) in enumerate(backward_tiles(b)):
            ks, qs = slice(k0, k0 + kl), slice(q0, q0 + ql)
            w = prob[h, b, ks, qs].astype(F32) * scal[h, b : b + 1, qs]
            gw = dot(vw[b, ks, :], gT[h, :, qs])
            gs = (w * (gw - scal[h, NB : NB + 1, qs])).astype(BF16)
            low = w.astype(BF16)
            into[1, ks, :] += dot(low, gn[qs, cols])
            into[0, ks, :] += dot(gs, qn[qs, cols])
            t = dot(kT[b, :, ks], gs)
            if b == 0 and n == 0:
                dqT[h, :, qs] = t
                dqT[h, :, HALF:] = jnp.zeros((HD, HALF), F32)
            else:
                dqT[h, :, qs] += t
        if b == NB - 1:
            dqn[:, cols] = (dqT[h] * SCALE).astype(BF16).T

    arrived(0)
    arrived(1)
    hop(4)
    prepare(4)
    hopped(4)
    hop(3)
    prepare(3)
    arrived(2)
    for h in range(GRP):
        qx[h, 0:HD, :] = qn[:, h * HD : h * HD + HD].T
    forward(4)
    hopped(3)
    hop(2)
    forward(3)
    prepare(2)
    hopped(2)
    hop(1)
    forward(2)
    prepare(1)
    forward(1)
    hopped(1)
    prepare(0)
    forward(0)

    arrived(3)
    for h in range(GRP):
        gT[h] = gn[:, h * HD : h * HD + HD].T

    def finish(h, _):
        inv = 1.0 / sums[h, 0:1, :]
        o = (acc[h] * inv).astype(BF16)
        scal[h, NB : NB + 1, :] = jnp.sum(
            o.astype(F32) * gT[h].astype(F32), axis=0, keepdims=True
        )
        for b in range(NB):
            scal[h, b : b + 1, :] = (
                jnp.exp2((maxes[h, b : b + 1, :] - maxes[h, NB : NB + 1, :]) * LOG2) * inv
            )
        on[:, aligned(h, HD)] = o.T
        return 0

    lax.fori_loop(0, GRP, finish, 0)

    slab = aligned(x, wide)
    tail = []
    for r in (1, 3, 2):
        copy = remote(
            on.at[aligned(peer_x[r], SH), :], att.at[:, slab], o_send.at[r], o_recv.at[r], peers[r]
        )
        copy.start()
        tail.append(copy)
    own = pltpu.make_async_copy(on.at[mine, :], att.at[:, slab], loc.at[4])
    own.start()
    tail.append(own)

    def pass_on(b):
        for n in range(2):
            total = dkv[n] * SCALE if n == 0 else dkv[n]
            if b > 0:
                reds[n, b - 1].wait()
                total = total + ring_in[b - 1, n].astype(F32)
            ring_out[b, n] = total.astype(BF16)
            reds[n, b] = remote(
                ring_out.at[b, n], ring_in.at[b, n], red_send.at[n, b], red_recv.at[n, b], down
            )
            reds[n, b].start()

    reds = {}
    for b in range(3):
        dkv[...] = jnp.zeros((2, BLK, HD), F32)

        def step(h, _, b=b):
            backward(b, h, dkv)
            return 0

        lax.fori_loop(0, GRP, step, 0)
        pass_on(b)
    dkv[...] = jnp.zeros((2, BLK, HD), F32)
    dkv_own[...] = jnp.zeros((2, BLK, HD), F32)
    part = wide // 2
    for half in range(2):
        first_head = half * (GRP // 2)

        def near(h, _):
            backward(3, h, dkv)
            return 0

        lax.fori_loop(first_head, first_head + GRP // 2, near, 0)
        if half == 1:
            pass_on(3)

        def nearest(h, _):
            backward(4, h, dkv_own)
            return 0

        lax.fori_loop(first_head, first_head + GRP // 2, nearest, 0)
        here = pl.ds(half * part, part)
        there = pl.ds(pl.multiple_of(x * wide + half * part, part), part)
        for r in (1, 3, 2):
            copy = remote(
                dqn.at[aligned(peer_x[r], SH), here], dq_out.at[:, there],
                dq_send.at[half, r], dq_recv.at[half, r], peers[r],
            )
            copy.start()
            tail.append(copy)
        own = pltpu.make_async_copy(dqn.at[mine, here], dq_out.at[:, there], loc.at[5 + half])
        own.start()
        tail.append(own)

    heads = aligned(x, HD)
    for n, out in enumerate((dk_out, dv_out)):
        total = dkv_own[n] * SCALE if n == 0 else dkv_own[n]
        reds[n, 3].wait()
        last[n] = (total + ring_in[3, n].astype(F32)).astype(BF16)
        for r in (1, 3, 2):
            copy = remote(
                last.at[n, aligned(peer_x[r], SH), :], out.at[:, heads],
                fin_send.at[n, r], fin_recv.at[n, r], peers[r],
            )
            copy.start()
            tail.append(copy)
        own = pltpu.make_async_copy(last.at[n, mine, :], out.at[:, heads], loc.at[7 + n])
        own.start()
        tail.append(own)
    for copy in tail:
        copy.wait()


def per_device(query_rows, key_rows, value_rows, grad_out, doc_lengths):
    anywhere = pl.BlockSpec(memory_space=pl.ANY)
    dma = pltpu.SemaphoreType.DMA
    wide = GRP * HD
    shapes = [query_rows.shape, query_rows.shape, key_rows.shape, value_rows.shape]
    return pl.pallas_call(
        kernel,
        out_shape=[jax.ShapeDtypeStruct(s, BF16) for s in shapes],
        in_specs=[pl.BlockSpec(memory_space=pltpu.SMEM)] + [anywhere] * 4,
        out_specs=[anywhere] * 4,
        scratch_shapes=[
            pltpu.VMEM((NB, BLK, HD), BF16),
            pltpu.VMEM((NB, BLK, HD), BF16),
            pltpu.VMEM((BLK, wide), BF16),
            pltpu.VMEM((BLK, wide), BF16),
            pltpu.VMEM((BLK, wide), BF16),
            pltpu.VMEM((BLK, wide), BF16),
            pltpu.VMEM((GRP, 2 * HD, BLK), BF16),
            pltpu.VMEM((GRP, HD, BLK), BF16),
            pltpu.VMEM((NB, BLK, 2 * HD), BF16),
            pltpu.VMEM((NB, HD, BLK), BF16),
            pltpu.VMEM((NB, HD + 16, BLK), BF16),
            pltpu.VMEM((GRP, NB, BLK, BLK), BF16),
            pltpu.VMEM((GRP, HD, BLK), F32),
            pltpu.VMEM((GRP, 8, BLK), F32),
            pltpu.VMEM((GRP, 8, BLK), F32),
            pltpu.VMEM((GRP, HD, BLK), F32),
            pltpu.VMEM((GRP, 8, BLK), F32),
            pltpu.VMEM((BLK, BLK), F32),
            pltpu.VMEM((BLK, BLK), F32),
            pltpu.VMEM((2, BLK, HD), F32),
            pltpu.VMEM((2, BLK, HD), F32),
            pltpu.VMEM((4, 2, BLK, HD), BF16),
            pltpu.VMEM((4, 2, BLK, HD), BF16),
            pltpu.VMEM((2, BLK, HD), BF16),
            dma((4, 4)),
            dma((4, 4)),
            dma((9,)),
            dma((2, 5)),
            dma((2, 5)),
            dma((4,)),
            dma((4,)),
            dma((2, 4)),
            dma((2, 4)),
            dma((2, 4)),
            dma((2, 4)),
            dma((2, 4)),
            dma((2, 4)),
        ],
        compiler_params=pltpu.CompilerParams(
            collective_id=0, has_side_effects=True, vmem_limit_bytes=60 * 1024 * 1024
        ),
    )(doc_lengths, query_rows, key_rows, value_rows, grad_out)


def solution(mesh):
    rows = P(("dp", "ulysses"), None)
    return jax.shard_map(
        per_device,
        mesh=mesh,
        in_specs=(rows, rows, rows, rows, P()),
        out_specs=(rows, rows, rows, rows),
        check_vma=False,
    )
```

time: 543 us -> 95.3 us (0.18)
  the two profiles are of different devices: /device:TPU:4 before, /device:TPU:16 now
where the time goes in v1:
time: 95.3 us; the launch traced here: 95 us
  Pallas kernels  89.4 us (94%)
  local copies, waits for them, and re-layouts  5.01 us (5%)
    pallas_call x1, Pallas kernels, per_device(): pl.pallas_call(kernel, out_shape=[jax.ShapeDtypeStruct(s, BF16) for s in...  89.4 us
    unnamed x10, local copies, waits for them, and re-layouts  5.01 us

profile of v1, /device:TPU:16, one launch (start us, length us, event | category | flops | bytes accessed | tf_op | source)
XLA Modules:
  0.0 95.0 jit_solution(15399660592034124787)
XLA Ops:
  0.6 89.4 %shard_map.84 = (bf16[128,4096]{1,0:T(8,128)(2,1)}, bf16[128,4096]{1,0:T(8,128)(2,1)}, bf16[128,512]{1,0:T(8,128)(2,1)}, bf16[128,512]{1,0:T(8,128)(2,1)}) custom-call(s32[16,12]{1,0:T(8,128)} %dl.1, bf16[128,4096]{1,0:T(8,128)(2,1)} %q_in.1, bf16[128,512]{1,0:T(8,128)(2,1)} %k_in.1, bf16[128,512]{1,0:T(8,128)(2,1)} %v_in.1, bf16[128,4096]{1,0:T(8,128)(2,1)} %g_in.1), custom_call_target="tpu_custom_call" | custom-call | tf_op jit(solution)/shard_map/pallas_call | solution.py:373
  90.0 0.0 copy-start
  90.0 2.4 %copy.13 = bf16[128,4096]{1,0:T(8,128)(2,1)} copy(bf16[128,4096]{1,0:T(8,128)(2,1)} %get-tuple-element.8) | data formatting | bytes 2097152
  92.4 0.0 copy-done
  92.4 0.0 copy-start.2
  92.4 1.0 %copy.14 = bf16[128,4096]{1,0:T(8,128)(2,1)} copy(bf16[128,4096]{1,0:T(8,128)(2,1)S(1)} %copy-done) | data formatting | bytes 2097152
  93.4 0.1 copy-done.2
  93.4 0.0 copy-start.1
  93.4 0.7 copy.15
  94.1 0.3 copy-done.1
  94.4 0.7 copy.16
Async XLA Ops:
  90.0 2.4 %copy-start = (bf16[128,4096]{1,0:T(8,128)(2,1)S(1)}, bf16[128,4096]{1,0:T(8,128)(2,1)}, u32[]{:S(2)}) copy-start(bf16[128,4096]{1,0:T(8,128)(2,1)} %get-tuple-element.9) | copy-start | bytes 3145732
  92.4 1.0 %copy-start.2 = (bf16[128,512]{1,0:T(8,128)(2,1)S(1)}, bf16[128,512]{1,0:T(8,128)(2,1)}, u32[]{:S(2)}) copy-start(bf16[128,512]{1,0:T(8,128)(2,1)} %get-tuple-element.10) | copy-start | bytes 393220
  93.4 1.0 %copy-start.1 = (bf16[128,512]{1,0:T(8,128)(2,1)S(1)}, bf16[128,512]{1,0:T(8,128)(2,1)}, u32[]{:S(2)}) copy-start(bf16[128,512]{1,0:T(8,128)(2,1)} %get-tuple-element.11) | copy-start | bytes 393220

commit v2 on v1

--- a/solution.py
+++ b/solution.py
@@ -54,7 +54,7 @@
     kw, vw, qn, gn, on, dqn,
     qx, gT, kx, kT, vTx, prob, acc, maxes, sums, dqT, scal, s_a, s_b,
     dkv, dkv_own, ring_in, ring_out, last,
-    in_send, in_recv, loc, hop_send, hop_recv, o_send, o_recv, dq_send, dq_recv,
+    in_send, in_recv, loc, hop_send, hop_recv, o_send, o_recv, dq_send, dq_recv, dq_loc,
     red_send, red_recv, fin_send, fin_recv,
 ):
     dp = lax.axis_index("dp")
@@ -79,24 +79,26 @@
 
     mine = aligned(x, SH)
     wide = GRP * HD
+    part = wide // 2
     moves = (
-        (k_in, HD, kw.at[NB - 1]),
-        (v_in, HD, vw.at[NB - 1]),
-        (q_in, wide, qn),
-        (g_in, wide, gn),
+        (k_in, HD, 0, HD, kw.at[NB - 1]),
+        (v_in, HD, 0, HD, vw.at[NB - 1]),
+        (q_in, wide, 0, part, qn),
+        (q_in, wide, part, part, qn),
+        (g_in, wide, 0, wide, gn),
     )
     arrive = []
     local = []
-    for n, (src, width, dst) in enumerate(moves):
+    for n, (src, step_by, skip, width, dst) in enumerate(moves):
         row = []
+        into = dst.at[mine, pl.ds(skip, width)]
         for r in (1, 3, 2):
-            copy = remote(
-                src.at[:, aligned(peer_x[r], width)], dst.at[mine, :],
-                in_send.at[n, r], in_recv.at[n, r], peers[r],
-            )
+            cols = pl.ds(pl.multiple_of(peer_x[r] * step_by + skip, HD), width)
+            copy = remote(src.at[:, cols], into, in_send.at[n, r], in_recv.at[n, r], peers[r])
             copy.start()
             row.append(copy)
-        own = pltpu.make_async_copy(src.at[:, aligned(x, width)], dst.at[mine, :], loc.at[n])
+        cols = pl.ds(pl.multiple_of(x * step_by + skip, HD), width)
+        own = pltpu.make_async_copy(src.at[:, cols], into, loc.at[n])
         own.start()
         arrive.append(row)
         local.append(own)
@@ -108,17 +110,17 @@
 
     hops = {}
 
-    def hop(b):
-        hops[b] = [
-            remote(w.at[b], w.at[b - 1], hop_send.at[n, b], hop_recv.at[n, b], up)
-            for n, w in enumerate((kw, vw))
-        ]
-        for copy in hops[b]:
-            copy.start()
-
-    def hopped(b):
-        for copy in hops[b]:
-            copy.wait()
+    windows = (kw, vw)
+
+    def hop(n, b):
+        w = windows[n]
+        hops[n, b] = remote(w.at[b], w.at[b - 1], hop_send.at[n, b], hop_recv.at[n, b], up)
+        hops[n, b].start()
+
+    def relay(n, b):
+        hops[n, b + 1].wait()
+        if b > 0:
+            hop(n, b)
 
     base = (z - (NB - 1)) * BLK
     lane = lax.broadcasted_iota(jnp.int32, (1, HD), 1)
@@ -141,11 +143,13 @@
     for h in range(GRP):
         qx[h, HD:, :] = bias
 
-    def prepare(b):
+    def prepare_keys(b):
         j = lax.broadcasted_iota(jnp.int32, (BLK, HD), 0) + b * BLK
         kx[b, :, HD:] = jnp.where((j >= key_lo) & (j < key_hi), 1.0, 0.0).astype(BF16)
         kx[b, :, 0:HD] = kw[b]
         kT[b] = kw[b].T
+
+    def prepare_values(b):
         vTx[b, 0:HD, :] = vw[b].T
         vTx[b, HD:, :] = jnp.ones((16, BLK), BF16)
 
@@ -168,55 +172,43 @@
         for n in range(2):
             maxes[h, b : b + 1, n * HALF : n * HALF + HALF] = tops[n]
 
-    def forward(b):
+    def forward(b, h, now, later, ahead):
+        top = maxes[h, b : b + 1, :]
         tops = [None, None]
+        outs = [None, None]
+        held = None
         for c in range(4):
-            scores(b, 0, s_a, c, tops)
-        put_tops(b, 0, tops)
-
-        def one(h, now, later):
-            ahead = jnp.minimum(h + 1, GRP - 1)
-            top = maxes[h, b : b + 1, :]
-            tops = [None, None]
-            outs = [None, None]
-            held = None
-            for c in range(4):
-                scores(b, ahead, later, c, tops)
-                q0, q1 = query_range(b, c)
-                rows = slice(c * SH, c * SH + SH)
-                p = jnp.exp2((now[rows, q0:q1] - top[:, q0:q1]) * LOG2).astype(BF16)
-                prob[h, b, rows, q0:q1] = p
-                if c % 2:
-                    pair = jnp.concatenate([held, p], axis=0)
-                    t = dot(vTx[b, :, c * SH - SH : c * SH + SH], pair)
-                    for n, lo in enumerate((0, HALF)):
-                        if q0 <= lo and lo + HALF <= q1:
-                            part = t[:, lo - q0 : lo - q0 + HALF]
-                            outs[n] = part if outs[n] is None else outs[n] + part
-                held = p
-            put_tops(b, ahead, tops)
-            for n in range(2):
-                qs = slice(n * HALF, n * HALF + HALF)
-                out, total, peak = outs[n][0:HD], outs[n][HD : HD + 1], top[:, qs]
-                if b == NB - 1:
-                    maxes[h, NB : NB + 1, qs] = peak
-                    sums[h, 0:1, qs] = total
-                    acc[h, :, qs] = out
-                else:
-                    old = maxes[h, NB : NB + 1, qs]
-                    new = jnp.maximum(old, peak)
-                    keep = jnp.exp2((old - new) * LOG2)
-                    add = jnp.exp2((peak - new) * LOG2)
-                    maxes[h, NB : NB + 1, qs] = new
-                    sums[h, 0:1, qs] = sums[h, 0:1, qs] * keep + total * add
-                    acc[h, :, qs] = acc[h, :, qs] * keep + out * add
-
-        def two(pair, _):
-            one(pair * 2, s_a, s_b)
-            one(pair * 2 + 1, s_b, s_a)
-            return 0
-
-        lax.fori_loop(0, GRP // 2, two, 0)
+            if ahead is not None:
+                scores(*ahead, later, c, tops)
+            q0, q1 = query_range(b, c)
+            rows = slice(c * SH, c * SH + SH)
+            p = jnp.exp2((now[rows, q0:q1] - top[:, q0:q1]) * LOG2).astype(BF16)
+            prob[h, b, rows, q0:q1] = p
+            if c % 2:
+                pair = jnp.concatenate([held, p], axis=0)
+                t = dot(vTx[b, :, c * SH - SH : c * SH + SH], pair)
+                for n, lo in enumerate((0, HALF)):
+                    if q0 <= lo and lo + HALF <= q1:
+                        piece = t[:, lo - q0 : lo - q0 + HALF]
+                        outs[n] = piece if outs[n] is None else outs[n] + piece
+            held = p
+        if ahead is not None:
+            put_tops(*ahead, tops)
+        for n in range(2):
+            qs = slice(n * HALF, n * HALF + HALF)
+            out, total, peak = outs[n][0:HD], outs[n][HD : HD + 1], top[:, qs]
+            if b == NB - 1:
+                maxes[h, NB : NB + 1, qs] = peak
+                sums[h, 0:1, qs] = total
+                acc[h, :, qs] = out
+            else:
+                old = maxes[h, NB : NB + 1, qs]
+                new = jnp.maximum(old, peak)
+                keep = jnp.exp2((old - new) * LOG2)
+                add = jnp.exp2((peak - new) * LOG2)
+                maxes[h, NB : NB + 1, qs] = new
+                sums[h, 0:1, qs] = sums[h, 0:1, qs] * keep + total * add
+                acc[h, :, qs] = acc[h, :, qs] * keep + out * add
 
     def backward(b, h, into):
         cols = aligned(h, HD)
@@ -237,31 +229,44 @@
         if b == NB - 1:
             dqn[:, cols] = (dqT[h] * SCALE).astype(BF16).T
 
-    arrived(0)
-    arrived(1)
-    hop(4)
-    prepare(4)
-    hopped(4)
-    hop(3)
-    prepare(3)
-    arrived(2)
-    for h in range(GRP):
-        qx[h, 0:HD, :] = qn[:, h * HD : h * HD + HD].T
-    forward(4)
-    hopped(3)
-    hop(2)
-    forward(3)
-    prepare(2)
-    hopped(2)
-    hop(1)
-    forward(2)
-    prepare(1)
-    forward(1)
-    hopped(1)
-    prepare(0)
-    forward(0)
-
-    arrived(3)
+    def queries(half):
+        arrived(2 + half)
+        for h in range(half * 4, half * 4 + 4):
+            qx[h, 0:HD, :] = qn[:, h * HD : h * HD + HD].T
+
+    steps = [(b, h) for half in range(2) for b in (4, 3) for h in range(half * 4, half * 4 + 4)]
+    steps += [(b, h) for b in (2, 1, 0) for h in range(GRP)]
+    before = {
+        (3, 0): lambda: relay(0, 2),
+        (3, 3): lambda: (relay(1, 2), queries(1)),
+        (4, 6): lambda: (prepare_keys(2), prepare_values(2)),
+        (3, 4): lambda: relay(0, 1),
+        (3, 6): lambda: relay(1, 1),
+        (2, 5): lambda: (prepare_keys(1), prepare_values(1)),
+        (1, 7): lambda: (relay(0, 0), prepare_keys(0)),
+        (0, 0): lambda: (relay(1, 0), prepare_values(0)),
+    }
+    for n in range(2):
+        arrived(n)
+        hop(n, 4)
+    prepare_keys(4)
+    prepare_values(4)
+    for n in range(2):
+        relay(n, 3)
+    prepare_keys(3)
+    prepare_values(3)
+    queries(0)
+    tops = [None, None]
+    for c in range(4):
+        scores(4, 0, s_a, c, tops)
+    put_tops(4, 0, tops)
+    for i, (b, h) in enumerate(steps):
+        if (b, h) in before:
+            before[b, h]()
+        now, later = (s_a, s_b) if i % 2 == 0 else (s_b, s_a)
+        forward(b, h, now, later, steps[i + 1] if i + 1 < len(steps) else None)
+
+    arrived(4)
     for h in range(GRP):
         gT[h] = gn[:, h * HD : h * HD + HD].T
 
@@ -278,7 +283,7 @@
         on[:, aligned(h, HD)] = o.T
         return 0
 
-    lax.fori_loop(0, GRP, finish, 0)
+    lax.fori_loop(0, GRP, finish, 0, unroll=2)
 
     slab = aligned(x, wide)
     tail = []
@@ -288,63 +293,72 @@
         )
         copy.start()
         tail.append(copy)
-    own = pltpu.make_async_copy(on.at[mine, :], att.at[:, slab], loc.at[4])
+    own = pltpu.make_async_copy(on.at[mine, :], att.at[:, slab], loc.at[5])
     own.start()
     tail.append(own)
 
-    def pass_on(b):
-        for n in range(2):
-            total = dkv[n] * SCALE if n == 0 else dkv[n]
-            if b > 0:
-                reds[n, b - 1].wait()
-                total = total + ring_in[b - 1, n].astype(F32)
-            ring_out[b, n] = total.astype(BF16)
-            reds[n, b] = remote(
-                ring_out.at[b, n], ring_in.at[b, n], red_send.at[n, b], red_recv.at[n, b], down
-            )
-            reds[n, b].start()
-
     reds = {}
-    for b in range(3):
-        dkv[...] = jnp.zeros((2, BLK, HD), F32)
-
-        def step(h, _, b=b):
-            backward(b, h, dkv)
-            return 0
-
-        lax.fori_loop(0, GRP, step, 0)
-        pass_on(b)
-    dkv[...] = jnp.zeros((2, BLK, HD), F32)
-    dkv_own[...] = jnp.zeros((2, BLK, HD), F32)
-    part = wide // 2
-    for half in range(2):
-        first_head = half * (GRP // 2)
-
-        def near(h, _):
-            backward(3, h, dkv)
-            return 0
-
-        lax.fori_loop(first_head, first_head + GRP // 2, near, 0)
-        if half == 1:
-            pass_on(3)
-
-        def nearest(h, _):
-            backward(4, h, dkv_own)
-            return 0
-
-        lax.fori_loop(first_head, first_head + GRP // 2, nearest, 0)
-        here = pl.ds(half * part, part)
-        there = pl.ds(pl.multiple_of(x * wide + half * part, part), part)
+
+    def pass_on(n, b):
+        total = dkv[b % 2, n] * SCALE if n == 0 else dkv[b % 2, n]
+        if b > 0:
+            reds[n, b - 1].wait()
+            total = total + ring_in[b - 1, n].astype(F32)
+        ring_out[b, n] = total.astype(BF16)
+        reds[n, b] = remote(
+            ring_out.at[b, n], ring_in.at[b, n], red_send.at[n, b], red_recv.at[n, b], down
+        )
+        reds[n, b].start()
+
+    def send_queries(h, heads, tag):
+        here = pl.ds(h * HD, heads * HD)
+        there = pl.ds(pl.multiple_of(x * wide + h * HD, HD), heads * HD)
         for r in (1, 3, 2):
             copy = remote(
                 dqn.at[aligned(peer_x[r], SH), here], dq_out.at[:, there],
-                dq_send.at[half, r], dq_recv.at[half, r], peers[r],
+                dq_send.at[tag, r], dq_recv.at[tag, r], peers[r],
             )
             copy.start()
             tail.append(copy)
-        own = pltpu.make_async_copy(dqn.at[mine, here], dq_out.at[:, there], loc.at[5 + half])
+        own = pltpu.make_async_copy(dqn.at[mine, here], dq_out.at[:, there], dq_loc.at[tag])
         own.start()
         tail.append(own)
+
+    def run(b, start, stop):
+        into = dkv_own if b == NB - 1 else dkv.at[b % 2]
+
+        def step(h, _):
+            backward(b, h, into)
+            return 0
+
+        lax.fori_loop(start, stop, step, 0, unroll=4)
+
+    zero = jnp.zeros((2, BLK, HD), F32)
+    dkv[0] = zero
+    dkv_own[...] = zero
+    run(0, 0, GRP)
+    pass_on(0, 0)
+    pass_on(1, 0)
+    dkv[1] = zero
+    run(1, 0, GRP)
+    pass_on(0, 1)
+    dkv[0] = zero
+    run(2, 0, 4)
+    pass_on(1, 1)
+    run(2, 4, GRP)
+    pass_on(0, 2)
+    dkv[1] = zero
+    run(3, 0, 4)
+    pass_on(1, 2)
+    run(4, 0, 4)
+    send_queries(0, 4, 0)
+    run(3, 4, GRP)
+    pass_on(0, 3)
+    pass_on(1, 3)
+    for h in range(4, GRP):
+        backward(4, h, dkv_own)
+        if h % 2:
+            send_queries(h - 1, 2, h // 2 - 1)
 
     heads = aligned(x, HD)
     for n, out in enumerate((dk_out, dv_out)):
@@ -358,10 +372,19 @@
             )
             copy.start()
             tail.append(copy)
-        own = pltpu.make_async_copy(last.at[n, mine, :], out.at[:, heads], loc.at[7 + n])
+        own = pltpu.make_async_copy(last.at[n, mine, :], out.at[:, heads], loc.at[8 + n])
         own.start()
         tail.append(own)
     for copy in tail:
+        copy.wait()
+
+
+def hand_on(*refs):
+    done = refs[8]
+    copies = [pltpu.make_async_copy(refs[n], refs[4 + n], done.at[n]) for n in range(4)]
+    for copy in copies:
+        copy.start()
+    for copy in copies:
         copy.wait()
 
 
@@ -370,11 +393,11 @@
     dma = pltpu.SemaphoreType.DMA
     wide = GRP * HD
     shapes = [query_rows.shape, query_rows.shape, key_rows.shape, value_rows.shape]
-    return pl.pallas_call(
+    results = pl.pallas_call(
         kernel,
-        out_shape=[jax.ShapeDtypeStruct(s, BF16) for s in shapes],
+        out_shape=[pltpu.VMEM(s, BF16) for s in shapes],
         in_specs=[pl.BlockSpec(memory_space=pltpu.SMEM)] + [anywhere] * 4,
-        out_specs=[anywhere] * 4,
+        out_specs=[pl.BlockSpec(memory_space=pltpu.VMEM)] * 4,
         scratch_shapes=[
             pltpu.VMEM((NB, BLK, HD), BF16),
             pltpu.VMEM((NB, BLK, HD), BF16),
@@ -395,20 +418,21 @@
             pltpu.VMEM((GRP, 8, BLK), F32),
             pltpu.VMEM((BLK, BLK), F32),
             pltpu.VMEM((BLK, BLK), F32),
-            pltpu.VMEM((2, BLK, HD), F32),
+            pltpu.VMEM((2, 2, BLK, HD), F32),
             pltpu.VMEM((2, BLK, HD), F32),
             pltpu.VMEM((4, 2, BLK, HD), BF16),
             pltpu.VMEM((4, 2, BLK, HD), BF16),
             pltpu.VMEM((2, BLK, HD), BF16),
-            dma((4, 4)),
-            dma((4, 4)),
-            dma((9,)),
+            dma((5, 4)),
+            dma((5, 4)),
+            dma((10,)),
             dma((2, 5)),
             dma((2, 5)),
             dma((4,)),
             dma((4,)),
-            dma((2, 4)),
-            dma((2, 4)),
+            dma((3, 4)),
+            dma((3, 4)),
+            dma((3,)),
             dma((2, 4)),
             dma((2, 4)),
             dma((2, 4)),
@@ -418,6 +442,14 @@
             collective_id=0, has_side_effects=True, vmem_limit_bytes=60 * 1024 * 1024
         ),
     )(doc_lengths, query_rows, key_rows, value_rows, grad_out)
+    return pl.pallas_call(
+        hand_on,
+        out_shape=[jax.ShapeDtypeStruct(s, BF16) for s in shapes],
+        in_specs=[pl.BlockSpec(memory_space=pltpu.VMEM)] * 4,
+        out_specs=[anywhere] * 4,
+        scratch_shapes=[dma((4,))],
+        compiler_params=pltpu.CompilerParams(vmem_limit_bytes=1024 * 1024),
+    )(*results)
 
 
 def solution(mesh):

time: 95.3 us -> 84 us (0.88)
  the two profiles are of different devices: /device:TPU:16 before, /device:TPU:48 now
where the time goes in v2:
time: 84 us; the launch traced here: 83.9 us
  Pallas kernels  83 us (99%)
    pallas_call x1, Pallas kernels, per_device(): pl.pallas_call(kernel, out_shape=[pltpu.VMEM(s, BF16) for s in shapes], i...  81.6 us

profile of v2, /device:TPU:48, one launch (start us, length us, event | category | flops | bytes accessed | tf_op | source)
XLA Modules:
  0.0 83.9 jit_solution(12438974943984280054)
XLA Ops:
  0.6 81.6 %shard_map.84 = (bf16[128,4096]{1,0:T(8,128)(2,1)S(1)}, bf16[128,4096]{1,0:T(8,128)(2,1)S(1)}, bf16[128,512]{1,0:T(8,128)(2,1)S(1)}, bf16[128,512]{1,0:T(8,128)(2,1)S(1)}) custom-call(s32[16,12]{1,0:T(8,128)} %dl.1, bf16[128,4096]{1,0:T(8,128)(2,1)} %q_in.1, bf16[128,512]{1,0:T(8,128)(2,1)} %k_in.1, bf16[128,512]{1,0:T(8,128)(2,1)} %v_in.1, ...), custom_call_target="tpu_custom_call" | custom-call | tf_op jit(solution)/shard_map/pallas_call | solution.py:396
  82.3 1.4 %shard_map.85 = (bf16[128,4096]{1,0:T(8,128)(2,1)}, bf16[128,4096]{1,0:T(8,128)(2,1)}, bf16[128,512]{1,0:T(8,128)(2,1)}, bf16[128,512]{1,0:T(8,128)(2,1)}) custom-call(bf16[128,4096]{1,0:T(8,128)(2,1)S(1)} %get-tuple-element.8.refs_0_, bf16[128,4096]{1,0:T(8,128)(2,1)S(1)} %get-tuple-element.9.refs_1_, bf16[128,512]{1,0:T(8,128)(2,1)S(1)} %get-tuple-element.10.refs_2_, ...), custom_call_target="tpu_custom_call" | custom-call | tf_op jit(solution)/shard_map/pallas_call | solution.py:445
